TPU v7x, 256 devices: a whole 4x4x8 slice. The times are simulated.
256 devices in a mesh: ctx: 32 (over y, x, core), tp: 8 (over z).
Axes of the slice: x: 4, y: 4, z: 8, core: 2. Of those that a mesh axis runs over, the one named last changes fastest.
Arguments:
- queries: bfloat16 [1, 32768, 4096], P(None, 'ctx', 'tp'), may hold values from -6 to 6
- keys: bfloat16 [1, 32768, 1024], P(None, 'ctx', 'tp'), may hold values from -6 to 6
- values: bfloat16 [1, 32768, 1024], P(None, 'ctx', 'tp'), may hold values from -6 to 6
- gates: int32 [1, 64, 8, 3], P(None, 'ctx', 'tp'), may hold values from 0 to 63, as said below
- out_weight: bfloat16 [4096, 4096], P('tp'), may hold values from -0.09375 to 0.09375
Outputs:
- projected: bfloat16 [1, 32768, 4096], P(None, 'ctx', 'tp')
Inputs may be any that keep to these rules, and one draw needn't show every extreme that they name: `gates`: for each sequence and key-value head, the 6 entries of query blocks 2 c to 2 c + 1 name blocks of 6 different values of (block // 2).
All inputs are finite; a program needn't handle non-finite values.
Results may differ from a plain program's by a relative error of at most 0.015.
Values may be sent and summed in bfloat16 or wider, within the bound.
No kernel may reach another device: no remote copies, remote signals or barrier semaphores. Data moves between devices by JAX's collectives and lax.ppermute only.
A program may use at most 64 MiB of HBM per device.

v0:
```python
import math
import jax
import jax.numpy as jnp
from jax import lax
from jax.sharding import PartitionSpec as P

HD = 128
TOKB = 512
PICKS = 3


def per_device(queries, keys, values, gates, out_weight):
    seq_count, tok_dev, query_width = queries.shape
    kv_heads = keys.shape[2] // HD
    head_group = query_width // HD // kv_heads
    blocks_dev = tok_dev // TOKB
    block_count = seq_count * blocks_dev
    position = lax.axis_index("ctx")
    local_block = jnp.arange(block_count, dtype=jnp.int32) % blocks_dev
    global_block = position * blocks_dev + local_block
    query_blocks = queries.reshape(block_count, TOKB, kv_heads, head_group, HD)
    gate_local = gates.reshape(block_count, kv_heads, PICKS)
    causal = jnp.arange(TOKB)[:, None] >= jnp.arange(TOKB)[None, :]
    score_scale = HD ** (-0.5)
    own_keys = keys.reshape(block_count, TOKB, kv_heads, HD)
    own_values = values.reshape(block_count, TOKB, kv_heads, HD)
    scores = (
        jnp.einsum("nqhgd,nkhd->nhgqk", query_blocks, own_keys, preferred_element_type=jnp.float32)
        * score_scale
    )
    scores = jnp.where(causal, scores, -jnp.inf)
    largest = jnp.max(scores, axis=-1)
    raw_weights = jnp.exp(scores - largest[..., None])
    denominator = jnp.sum(raw_weights, axis=-1)
    weighted = jnp.einsum(
        "nhgqk,nkhd->nhgqd",
        raw_weights.astype(jnp.bfloat16),
        own_values,
        preferred_element_type=jnp.float32,
    )
    key_piece = lax.all_gather(keys, "ctx", axis=1, tiled=True)
    value_piece = lax.all_gather(values, "ctx", axis=1, tiled=True)
    piece_rows = key_piece.shape[1]
    step_rows = math.gcd(piece_rows, TOKB)

    def visit(step_index, carried):
        first_row = step_index * step_rows
        key_sub = lax.dynamic_slice_in_dim(key_piece, step_index * step_rows, step_rows, 1)
        value_sub = lax.dynamic_slice_in_dim(value_piece, step_index * step_rows, step_rows, 1)
        block_index = first_row // TOKB
        chosen = jnp.any(gate_local == block_index, axis=2) & (block_index < global_block)[:, None]

        def update(current):
            run_max, run_total, run_weighted = current
            key_rows = jnp.repeat(key_sub, blocks_dev, axis=0).reshape(
                block_count, step_rows, kv_heads, HD
            )
            value_rows = jnp.repeat(value_sub, blocks_dev, axis=0).reshape(
                block_count, step_rows, kv_heads, HD
            )
            piece_scores = (
                jnp.einsum(
                    "nqhgd,nkhd->nhgqk", query_blocks, key_rows, preferred_element_type=jnp.float32
                )
                * score_scale
            )
            piece_scores = jnp.where(chosen[:, :, None, None, None], piece_scores, -jnp.inf)
            new_max = jnp.maximum(run_max, jnp.max(piece_scores, axis=-1))
            rescale = jnp.exp(run_max - new_max)
            new_weights = jnp.exp(piece_scores - new_max[..., None])
            new_total = run_total * rescale + jnp.sum(new_weights, axis=-1)
            added = jnp.einsum(
                "nhgqk,nkhd->nhgqd",
                new_weights.astype(jnp.bfloat16),
                value_rows,
                preferred_element_type=jnp.float32,
            )
            return (new_max, new_total, run_weighted * rescale[..., None] + added)

        return lax.cond(jnp.any(chosen), update, lambda current: current, carried)

    run_max, run_total, run_weighted = lax.fori_loop(
        0, piece_rows // step_rows, visit, (largest, denominator, weighted)
    )
    attended = (run_weighted / run_total[..., None]).astype(jnp.bfloat16)
    attended = jnp.transpose(attended, (0, 3, 1, 2, 4)).reshape(seq_count, tok_dev, query_width)
    partial_terms = jnp.dot(
        attended.reshape(-1, query_width), out_weight, preferred_element_type=jnp.float32
    )
    partial_terms = partial_terms.astype(jnp.bfloat16).reshape(
        seq_count, tok_dev, out_weight.shape[1]
    )
    return (
        lax.psum_scatter(partial_terms, "tp", scatter_dimension=2, tiled=True)
        .astype(jnp.float32)
        .astype(jnp.bfloat16)
    )


def solution(mesh):
    placed = (
        P(None, "ctx", "tp"),
        P(None, "ctx", "tp"),
        P(None, "ctx", "tp"),
        P(None, "ctx", "tp", None),
        P("tp", None),
    )
    return jax.shard_map(
        per_device, mesh=mesh, in_specs=placed, out_specs=P(None, "ctx", "tp"), check_vma=False
    )
```

profile of v0, /device:TPU:1, one launch (start us, length us, event | category | flops | bytes accessed | tf_op | source)
XLA Modules:
  0.0 382.9 jit_solution(16034697490817509006)
XLA Ops:
  6.5 0.7 all-gather.3.cloned.1.call-update
  7.3 0.7 all-gather.5.cloned.1.call-update
  8.1 1.3 reshape.133
  9.4 1.3 reshape.137
  11.0 2.5 fusion.23
  13.5 1.7 fusion.22
  15.3 2.6 fusion.28
  17.9 54.0 %all-gather.3.cloned.1.call-done = bf16[1,32768,128]{2,1,0:T(8,128)(2,1)} async-done(((bf16[1,1024,128]{2,1,0:T(8,128)(2,1)}), bf16[1,32768,128]{2,1,0:T(8,128)(2,1)}) %all-gather.3.cloned.1.call-update) | async-done | bytes 8388624 | tf_op jit(solution)/shard_map/all_gather | solution.py:41
  71.9 60.0 %all-gather.5.cloned.1.call-done = bf16[1,32768,128]{2,1,0:T(8,128)(2,1)} async-done(((bf16[1,1024,128]{2,1,0:T(8,128)(2,1)}), bf16[1,32768,128]{2,1,0:T(8,128)(2,1)}) %all-gather.5.cloned.1.call-update) | async-done | bytes 8388624 | tf_op jit(solution)/shard_map/all_gather | solution.py:42
  131.9 102.1 %while.20 = (s32[]{:T(128)}, f32[2,1,4,512]{3,2,0,1:T(4,128)S(1)}, f32[2,1,4,512]{3,2,0,1:T(4,128)S(1)}, f32[2,1,4,512,128]{4,3,2,0,1:T(8,128)S(1)}, s32[2,1,3]{...) while((s32[]{:T(128)}, f32[2,1,4,512]{3,2,0,1:T(4,128)S(1)}, ...), condition=%wide.region_9.10_spmd.clone, body=%wide.region_2.9_spmd.clone.sunk | while | flops 1097871360 | bytes 31457836 | solution.py:82
  132.1 0.7 and_reduce_fusion.2
  133.5 0.7 and_reduce_fusion.2
  134.8 7.5 %conditional.3 = ((f32[2,1,4,512]{3,2,0,1:T(4,128)S(1)}, f32[2,1,4,512]{3,2,0,1:T(4,128)S(1)}, f32[2,1,4,512,128]{4,3,2,0,1:T(8,128)S(1)})) conditional(s32[]{:T(128)} %convert_element_type.48, (f32[2,1,4,512]{3,2,0,1:T(4,128)S(1)}, f32[2,1,4,512]{3,2,0,1:T(4,128)S(1)}, f32[2,1,4,512,128]{4,3,2,0,1:T(8,128)S(1)}) %tuple.65, (s32[]{:T(128)}, ...), branch_computations={%region_5.5_spmd, %region_6.8_spmd} | conditional | flops 1097871360 | bytes 31457362 | solution.py:80
  134.9 1.0 dynamic-slice_bitcast_fusion
  135.9 1.3 bitcast_reduce_fusion
  137.2 3.4 bitcast_add_fusion
  140.6 1.7 fusion.4
  142.5 0.7 and_reduce_fusion.2
  144.0 0.7 and_reduce_fusion.2
  145.5 0.7 and_reduce_fusion.2
  147.0 0.7 and_reduce_fusion.2
  148.5 0.7 and_reduce_fusion.2
  149.9 0.7 and_reduce_fusion.2
  151.4 0.7 and_reduce_fusion.2
  152.9 0.7 and_reduce_fusion.2
  154.4 0.7 and_reduce_fusion.2
  155.8 0.7 and_reduce_fusion.2
  157.3 0.7 and_reduce_fusion.2
  158.8 0.7 and_reduce_fusion.2
  160.3 0.7 and_reduce_fusion.2
  161.8 0.7 and_reduce_fusion.2
  163.2 0.7 and_reduce_fusion.2
  164.7 0.7 and_reduce_fusion.2
  166.2 0.7 and_reduce_fusion.2
  167.7 0.7 and_reduce_fusion.2
  169.2 0.7 and_reduce_fusion.2
  170.6 0.7 and_reduce_fusion.2
  172.1 0.7 and_reduce_fusion.2
  173.6 0.7 and_reduce_fusion.2
  175.1 0.7 and_reduce_fusion.2
  176.6 0.7 and_reduce_fusion.2
  178.0 0.7 and_reduce_fusion.2
  189.9 0.7 and_reduce_fusion.2
  218.0 0.7 and_reduce_fusion.2
  234.1 0.7 fusion.35
  234.8 0.8 copy.15
  235.6 8.9 %convert_bitcast_fusion = bf16[1,1024,4096]{2,1,0:T(8,128)(2,1)} fusion(bf16[512,4096]{1,0:T(8,128)(2,1)} %param.13, bf16[128,8,4,128]{3,2,1,0:T(4,128)(2,1)S(1)} %bitcast.116), kind=kOutput, calls=%fused_computation.31 | convolution fusion | flops 4299161600 | bytes 13631488 | tf_op jit(solution)/shard_map/dot_general | solution.py:87
  244.6 131.8 %reduce-scatter.2.cloned.1.call-done = bf16[1,1024,512]{2,1,0:T(8,128)(2,1)} async-done(((bf16[1,1024,4096]{2,1,0:T(8,128)(2,1)}), bf16[1,1024,512]{2,1,0:T(8,128)(2,1)}) %reduce-scatter.2.cloned.1.call-update) | async-done | bytes 1048592 | tf_op jit(solution)/shard_map/reduce_scatter | solution.py:94
  (240 shorter events, 32.8 us)
Async XLA Ops:
  6.5 65.4 %all-gather.3.cloned.1.call-start = ((), (), s32[]{:S(2)}) async-start(), calls=%async_computation.1 | async-start | bytes 8650752 | tf_op jit(solution)/shard_map/all_gather | solution.py:41
  7.3 124.7 %all-gather.5.cloned.1.call-start = ((), (), s32[]{:S(2)}) async-start(), calls=%async_computation.2 | async-start | bytes 8650752 | tf_op jit(solution)/shard_map/all_gather | solution.py:42
  8.0 368.4 %reduce-scatter.2.cloned.1.call-start = ((), (), s32[]{:S(2)}) async-start(), calls=%async_computation.3 | async-start | bytes 9437184 | tf_op jit(solution)/shard_map/reduce_scatter | solution.py:94
  11.0 4.3 %copy-start = (bf16[1,1024,128]{2,1,0:T(8,128)(2,1)S(1)}, bf16[1,1024,128]{2,1,0:T(8,128)(2,1)}, u32[]{:S(2)}) copy-start(bf16[1,1024,128]{2,1,0:T(8,128)(2,1)} %param.11) | copy-start | bytes 786436
  15.3 116.6 %copy-start.1 = (s32[1,2,1,3]{3,2,1,0:T(1,128)S(1)}, s32[1,2,1,3]{3,2,1,0:T(1,128)}, u32[]{:S(2)}) copy-start(s32[1,2,1,3]{3,2,1,0:T(1,128)} %param.12) | copy-start | bytes 76
Sparse Core Ops, SparseCore 0:
  9.9 61.9 all-gather.2
  74.5 57.4 all-gather.4
  244.7 131.6 reduce-scatter.1
where the time goes:
time: 384 us; the launch traced here: 383 us
  waiting for transfers between devices  247 us (64%)
  other arithmetic  55.4 us (14%)
  loops' own time  43.6 us (11%)
  matrix products  18.7 us (5%)
  between operations  13.2 us (3%)
  local copies, waits for them, and re-layouts  4.65 us (1%)
    reduce_scatter x1, waiting for transfers between devices, per_device(): lax.psum_scatter(partial_terms, 'tp', scatter_dimension=2, tiled=True)  132 us
    all_gather x1, waiting for transfers between devices, per_device(): value_piece = lax.all_gather(values, 'ctx', axis=1, tiled=True)  60 us
    all_gather x1, waiting for transfers between devices, per_device(): key_piece = lax.all_gather(keys, 'ctx', axis=1, tiled=True)  54 us
    reduce_or x64, other arithmetic, visit(): return lax.cond(jnp.any(chosen), update, lambda current: current, carried)  42.8 us
    another operation x1, loops' own time, per_device(): lax.fori_loop(0, piece_rows // step_rows, visit, (largest, denominator, w...  42.8 us
    dot_general x1, matrix products, per_device(): jnp.dot(attended.reshape(-1, query_width), out_weight, preferred_element_...  8.92 us
    reduce_or x64, other arithmetic, visit(): jnp.any(gate_local == block_index, axis=2)  7.78 us
  transfers between devices with their start and end apart: 3, of which 3 were waited for; matrix products, arithmetic and copies ran while one was open for 3% of the time, Pallas kernels for 0%

commit v1 on v0

--- a/solution.py
+++ b/solution.py
@@ -39,7 +39,10 @@
         preferred_element_type=jnp.float32,
     )
     key_piece = lax.all_gather(keys, "ctx", axis=1, tiled=True)
-    value_piece = lax.all_gather(values, "ctx", axis=1, tiled=True)
+    count = lax.axis_size("ctx")
+    blocks = jnp.stack([values for _ in range(count)])
+    blocks = lax.all_to_all(blocks, "ctx", split_axis=0, concat_axis=0)
+    value_piece = jnp.concatenate(blocks, axis=1)
     piece_rows = key_piece.shape[1]
     step_rows = math.gcd(piece_rows, TOKB)
 

time: 384 us -> 396 us (1.031)
  starting transfers between devices: 0.08 us -> 8.81 us
    all_to_all x0 -> x1, waiting for transfers between devices: none -> 104 us  [per_device(): blocks = lax.all_to_all(blocks, 'ctx', split_axis=0, concat_axis=0)]
    all_gather x1 -> x0, waiting for transfers between devices: 60 us -> none  [per_device(): value_piece = lax.all_gather(values, 'ctx', axis=1, tiled=True)]
    all_gather x1, waiting for transfers between devices: 54 us -> 7.48 us  [per_device(): key_piece = lax.all_gather(keys, 'ctx', axis=1, tiled=True)]
    all_to_all x0 -> x1, starting transfers between devices: none -> 8.76 us  [per_device(): blocks = lax.all_to_all(blocks, 'ctx', split_axis=0, concat_axis=0)]
    another operation x2 -> x3, local copies, waits for them, and re-layouts: 2.34 us -> 7.34 us  [the longest x1 6.06 us: per_device(): blocks = jnp.stack([values for _ in range(count)])]
where the time goes in v1:
time: 396 us; the launch traced here: 395 us
  waiting for transfers between devices  247 us (62%)
  other arithmetic  54.3 us (14%)
  loops' own time  44.6 us (11%)
  matrix products  17.9 us (5%)
  between operations  13.5 us (3%)
  starting transfers between devices  8.81 us (2%)
  local copies, waits for them, and re-layouts  8.6 us (2%)
    reduce_scatter x1, waiting for transfers between devices, per_device(): lax.psum_scatter(partial_terms, 'tp', scatter_dimension=2, tiled=True)  135 us
    all_to_all x1, waiting for transfers between devices, per_device(): blocks = lax.all_to_all(blocks, 'ctx', split_axis=0, concat_axis=0)  104 us
    another operation x1, loops' own time, per_device(): lax.fori_loop(0, piece_rows // step_rows, visit, (largest, denominator, w...  43.8 us
    reduce_or x64, other arithmetic, visit(): return lax.cond(jnp.any(chosen), update, lambda current: current, carried)  41.7 us
    dot_general x1, matrix products, per_device(): jnp.dot(attended.reshape(-1, query_width), out_weight, preferred_element_...  8.91 us
    all_to_all x1, starting transfers between devices, per_device(): blocks = lax.all_to_all(blocks, 'ctx', split_axis=0, concat_axis=0)  8.76 us
  transfers between devices with their start and end apart: 3, of which 3 were waited for; matrix products, arithmetic and copies ran while one was open for 3% of the time, Pallas kernels for 0%

profile of v1, /device:TPU:1, one launch (start us, length us, event | category | flops | bytes accessed | tf_op | source)
XLA Modules:
  0.0 394.9 jit_solution(6888350748640488151)
XLA Ops:
  6.5 0.7 all-gather.2.cloned.1.call-update
  7.3 6.1 %stack.2 = bf16[32,1,1024,128]{3,2,1,0:T(8,128)(2,1)} broadcast(bf16[1024,128]{1,0:T(8,128)(2,1)} %bitcast.121), dimensions={2,3} | broadcast | bytes 8650752 | tf_op jit(solution)/shard_map/stack | solution.py:43
  13.3 8.8 %all-to-all-start = ((bf16[32,1,1024,128]{3,2,1,0:T(8,128)(2,1)}), bf16[32,1,1024,128]{3,2,1,0:T(8,128)(2,1)}, u32[]{:S(2)}, u32[]{:S(2)}) async-start(bf16[32,1,1024,128]{3,2,1,0:T(8,128)(2,1)} %stack.2), calls=%async_computation | async-start | bytes 16777216 | tf_op jit(solution)/shard_map/all_to_all | solution.py:44
  23.0 1.8 fusion.23
  24.8 1.7 fusion.22
  26.6 2.5 fusion.28
  29.1 104.0 %all-to-all-done = bf16[32,1,1024,128]{3,2,1,0:T(8,128)(2,1)} async-done(((bf16[32,1,1024,128]{3,2,1,0:T(8,128)(2,1)}), bf16[32,1,1024,128]{3,2,1,0:T(8,128)(2,1)}, u32[]{:S(2)}, u32[]{:S(2)}) %all-to-all-start) | async-done | bytes 8388640 | tf_op jit(solution)/shard_map/all_to_all | solution.py:44
  133.1 7.5 %all-gather.2.cloned.1.call-done = bf16[1,32768,128]{2,1,0:T(8,128)(2,1)} async-done(((bf16[1,1024,128]{2,1,0:T(8,128)(2,1)}), bf16[1,32768,128]{2,1,0:T(8,128)(2,1)}) %all-gather.2.cloned.1.call-update) | async-done | bytes 8388624 | tf_op jit(solution)/shard_map/all_gather | solution.py:41
  140.6 102.0 %while.20 = (s32[]{:T(128)}, f32[2,1,4,512]{3,2,0,1:T(4,128)S(1)}, f32[2,1,4,512]{3,2,0,1:T(4,128)S(1)}, f32[2,1,4,512,128]{4,3,2,0,1:T(8,128)S(1)}, s32[2,1,3]{...) while((s32[]{:T(128)}, f32[2,1,4,512]{3,2,0,1:T(4,128)S(1)}, ...), condition=%wide.region_9.10_spmd.clone, body=%wide.region_2.9_spmd.clone.sunk | while | flops 1097871360 | bytes 31457836 | solution.py:85
  143.5 7.5 %conditional.3 = ((f32[2,1,4,512]{3,2,0,1:T(4,128)S(1)}, f32[2,1,4,512]{3,2,0,1:T(4,128)S(1)}, f32[2,1,4,512,128]{4,3,2,0,1:T(8,128)S(1)})) conditional(s32[]{:T(128)} %convert_element_type.48, (f32[2,1,4,512]{3,2,0,1:T(4,128)S(1)}, f32[2,1,4,512]{3,2,0,1:T(4,128)S(1)}, f32[2,1,4,512,128]{4,3,2,0,1:T(8,128)S(1)}) %tuple.66, (s32[]{:T(128)}, ...), branch_computations={%region_5.5_spmd, %region_6.8_spmd} | conditional | flops 1097871360 | bytes 31457362 | solution.py:83
  143.5 1.0 dynamic-slice_bitcast_fusion
  144.5 1.3 bitcast_reduce_fusion
  145.8 3.4 bitcast_add_fusion
  149.2 1.7 fusion.4
  152.7 0.7 and_reduce_fusion.2
  154.1 0.7 and_reduce_fusion.2
  155.6 0.7 and_reduce_fusion.2
  157.1 0.7 and_reduce_fusion.2
  158.6 0.7 and_reduce_fusion.2
  160.0 0.7 and_reduce_fusion.2
  167.4 0.7 and_reduce_fusion.2
  168.9 0.7 and_reduce_fusion.2
  170.4 0.7 and_reduce_fusion.2
  171.9 0.7 and_reduce_fusion.2
  173.3 0.7 and_reduce_fusion.2
  174.8 0.7 and_reduce_fusion.2
  180.7 0.7 and_reduce_fusion.2
  182.2 0.7 and_reduce_fusion.2
  183.7 0.7 and_reduce_fusion.2
  185.1 0.7 and_reduce_fusion.2
  186.6 0.7 and_reduce_fusion.2
  188.1 0.7 and_reduce_fusion.2
  195.5 0.7 and_reduce_fusion.2
  197.0 0.7 and_reduce_fusion.2
  198.4 0.7 and_reduce_fusion.2
  199.9 0.7 and_reduce_fusion.2
  201.4 0.7 and_reduce_fusion.2
  202.9 0.7 and_reduce_fusion.2
  208.8 0.7 and_reduce_fusion.2
  210.2 0.7 and_reduce_fusion.2
  211.7 0.7 and_reduce_fusion.2
  213.2 0.7 and_reduce_fusion.2
  214.7 0.7 and_reduce_fusion.2
  216.2 0.7 and_reduce_fusion.2
  242.6 0.7 fusion.35
  243.3 0.8 copy.21
  244.1 8.9 %convert_bitcast_fusion = bf16[1,1024,4096]{2,1,0:T(8,128)(2,1)} fusion(bf16[512,4096]{1,0:T(8,128)(2,1)} %param.13, bf16[128,8,4,128]{3,2,1,0:T(4,128)(2,1)S(1)} %bitcast.118), kind=kOutput, calls=%fused_computation.31 | convolution fusion | flops 4299161600 | bytes 13631488 | tf_op jit(solution)/shard_map/dot_general | solution.py:90
  253.1 135.0 %reduce-scatter.2.cloned.1.call-done = bf16[1,1024,512]{2,1,0:T(8,128)(2,1)} async-done(((bf16[1,1024,4096]{2,1,0:T(8,128)(2,1)}), bf16[1,1024,512]{2,1,0:T(8,128)(2,1)}) %reduce-scatter.2.cloned.1.call-update) | async-done | bytes 1048592 | tf_op jit(solution)/shard_map/reduce_scatter | solution.py:97
  (244 shorter events, 32.1 us)
Async XLA Ops:
  6.5 134.0 %all-gather.2.cloned.1.call-start = ((), (), s32[]{:S(2)}) async-start(), calls=%async_computation.2 | async-start | bytes 8650752 | tf_op jit(solution)/shard_map/all_gather | solution.py:41
  13.3 8.8 %copy-start = (bf16[1,1024,512]{2,1,0:T(8,128)(2,1)S(1)}, bf16[1,1024,512]{2,1,0:T(8,128)(2,1)}, u32[]{:S(2)}) copy-start(bf16[1,1024,512]{2,1,0:T(8,128)(2,1)} %param.9) | copy-start | bytes 3145732
  13.3 9.7 %copy-start.1 = (bf16[1,1024,128]{2,1,0:T(8,128)(2,1)S(1)}, bf16[1,1024,128]{2,1,0:T(8,128)(2,1)}, u32[]{:S(2)}) copy-start(bf16[1,1024,128]{2,1,0:T(8,128)(2,1)} %param.10) | copy-start | bytes 786436
  13.3 119.8 %all-to-all-start = ((bf16[32,1,1024,128]{3,2,1,0:T(8,128)(2,1)}), bf16[32,1,1024,128]{3,2,1,0:T(8,128)(2,1)}, u32[]{:S(2)}, u32[]{:S(2)}) async-start(bf16[32,1,1024,128]{3,2,1,0:T(8,128)(2,1)} %stack.2), calls=%async_computation | async-start | bytes 16777216 | tf_op jit(solution)/shard_map/all_to_all | solution.py:44
  22.1 366.0 %reduce-scatter.2.cloned.1.call-start = ((), (), s32[]{:S(2)}) async-start(), calls=%async_computation.3 | async-start | bytes 9437184 | tf_op jit(solution)/shard_map/reduce_scatter | solution.py:97
  23.0 3.6 copy-start.2
  26.5 114.0 %copy-start.3 = (s32[1,2,1,3]{3,2,1,0:T(1,128)S(1)}, s32[1,2,1,3]{3,2,1,0:T(1,128)}, u32[]{:S(2)}) copy-start(s32[1,2,1,3]{3,2,1,0:T(1,128)} %param.12) | copy-start | bytes 76
Sparse Core Ops, SparseCore 0:
  9.9 130.6 all-gather.1
  253.2 134.8 reduce-scatter.1
